TPU v7x, 256 devices: a whole 4x4x8 slice. The times are simulated.
256 devices in a mesh: rows: 8 (over x, core), pts: 32 (over y, z).
Axes of the slice: x: 4, y: 4, z: 8, core: 2. Of those that a mesh axis runs over, the one named last changes fastest.
Arguments:
- features: bfloat16 [32768, 128], P('pts'), may hold values from -6 to 6
- targets: bfloat16 [32768, 256], P('pts'), may hold values from -6 to 6
- coefficients: float32 [32768, 256], P('pts'), may hold values from -6 to 6
- momentum: float32 [32768, 256], P('pts'), may hold values from -6 to 6
- block_index: int32 [2, 2048], replicated, may hold values from 0 to 32767, as said below
- pivot_index: int32 [2, 512], replicated, may hold values from 0 to 2047, as said below
- nystrom_core: bfloat16 [2, 512, 512], replicated, may hold values from -0.5 to 3
Outputs:
- new_coefficients: float32 [32768, 256], P('pts')
- new_momentum: float32 [32768, 256], P('pts')
Inputs may be any that keep to these rules, and one draw needn't show every extreme that they name: `block_index`: each row lists 2048 distinct points; a point p belongs to index p // 1024 of pts; in each row one index of pts, drawn from the seed, owns exactly 24 of the points in every aligned group of 256 positions, and no index owns more than 24 points of any such group. `pivot_index`: each row lists 512 distinct positions.
All inputs are finite; a program needn't handle non-finite values.
Results may differ from a plain program's by a relative error of at most 0.0041.
The roundings to bfloat16 on the way count: a program that leaves them out, or rounds other values in their place, can miss the bound.
Values may be sent and summed in bfloat16 or wider, within the bound.
A program may use at most 64 MiB of HBM per device.

v0:
```python
import jax
import jax.numpy as jnp
from jax import lax
from jax.sharding import PartitionSpec as P

UPDATES = 2
alpha_mix = 0.6
beta_keep = 0.9
step_size = 0.2
momentum_gain = 1.5
ridge_term = 1.0


def kernel_tile(left_rows, right_rows):
    inner_prod = lax.dot_general(
        left_rows, right_rows, (((1,), (1,)), ((), ())), preferred_element_type=jnp.float32
    )
    left_sq = jnp.sum(jnp.square(left_rows.astype(jnp.float32)), axis=1)
    right_sq = jnp.sum(jnp.square(right_rows.astype(jnp.float32)), axis=1)
    squared = left_sq[:, None] + right_sq[None, :] - 2.0 * inner_prod
    return jnp.exp(squared * (-3.5 / left_rows.shape[1])).astype(jnp.bfloat16)


def project_rows(factor, resid):
    return lax.dot_general(
        factor,
        resid.astype(jnp.bfloat16),
        (((0,), (0,)), ((), ())),
        preferred_element_type=jnp.float32,
    )


def finish_step(resid, factor, proj, core_now):
    lifted = jnp.dot(
        core_now, proj.astype(jnp.bfloat16), preferred_element_type=jnp.float32
    ).astype(jnp.bfloat16)
    return (resid - jnp.dot(factor, lifted, preferred_element_type=jnp.float32)).astype(
        jnp.bfloat16
    )


def owned_rows(local_feats, wanted, first_point):
    local_pos = wanted - first_point
    holder = (local_pos >= 0) & (local_pos < local_feats.shape[0])
    safe_pos = jnp.clip(local_pos, 0, local_feats.shape[0] - 1)
    return (holder, safe_pos)


def shards(features, targets, coefficients, momentum, block_index, pivot_index, nystrom_core):
    row_count = lax.axis_size("rows")
    pts_count = lax.axis_size("pts")
    row_id = lax.axis_index("rows")
    pts_id = lax.axis_index("pts")
    local_points = features.shape[0]
    per_row = block_index.shape[1] // row_count
    per_device = per_row // pts_count
    first_point = pts_id * local_points
    current = coefficients
    momentum_now = momentum
    for update in range(UPDATES):
        mixed = alpha_mix * momentum_now + (1.0 - alpha_mix) * current
        mixed_bf = mixed.astype(jnp.bfloat16)
        whole_index = block_index[update]
        row_points = lax.dynamic_slice_in_dim(whole_index, row_id * per_row, per_row)
        holder, safe_pos = owned_rows(features, row_points, first_point)
        row_terms = jnp.where(holder[:, None], features[safe_pos], jnp.zeros((), jnp.bfloat16))
        offset = jnp.where(
            holder[:, None],
            ridge_term * mixed[safe_pos] - targets[safe_pos].astype(jnp.float32),
            0.0,
        )
        pivot_points = whole_index[pivot_index[update]]
        pivot_holder, pivot_pos = owned_rows(features, pivot_points, first_point)
        pivot_terms = jnp.where(
            pivot_holder[:, None], features[pivot_pos], jnp.zeros((), jnp.bfloat16)
        )
        got_rows, got_pivots = (
            lax.psum(row_terms, "pts").astype(jnp.float32),
            lax.psum(pivot_terms, "pts").astype(jnp.float32),
        )
        block_feats = got_rows.astype(jnp.bfloat16)
        pivot_feats = got_pivots.astype(jnp.bfloat16)
        partial_value = (
            jnp.dot(
                kernel_tile(block_feats, features), mixed_bf, preferred_element_type=jnp.float32
            )
            + offset
        )
        local_all = whole_index - first_point
        whole_slots = jnp.where(
            (local_all >= 0) & (local_all < local_points), local_all, local_points
        )
        resid = lax.psum_scatter(partial_value, "pts", scatter_dimension=0, tiled=True)
        share_feats = lax.dynamic_slice_in_dim(block_feats, pts_id * per_device, per_device)
        factor = kernel_tile(share_feats, pivot_feats)
        proj = lax.psum(project_rows(factor, resid), ("rows", "pts"))
        step_bf = finish_step(resid, factor, proj, nystrom_core[update])
        steps = lax.all_gather(step_bf, ("rows", "pts"), axis=0, tiled=True)
        change = steps.astype(jnp.float32)
        current = mixed.at[whole_slots].add(-step_size * change, mode="drop")
        momentum_now = (
            (beta_keep * momentum_now + (1.0 - beta_keep) * mixed)
            .at[whole_slots]
            .add(-step_size * momentum_gain * change, mode="drop")
        )
    return (current, momentum_now)


def solution(mesh):
    in_specs = (P("pts", None), P("pts", None), P("pts", None), P("pts", None), P(), P(), P())
    out_specs = (P("pts", None), P("pts", None))
    return jax.shard_map(shards, mesh=mesh, in_specs=in_specs, out_specs=out_specs, check_vma=False)
```

profile of v0, /device:TPU:1, one launch (start us, length us, event | category | flops | bytes accessed | tf_op | source)
XLA Modules:
  0.0 1027.0 jit_solution(4563416117021022142)
XLA Ops:
  7.2 0.8 fusion.70
  8.1 0.8 compare_select_fusion.3
  8.9 3.1 gather_fusion.8
  12.1 3.1 gather_fusion.3
  15.3 0.9 gather_fusion
  16.2 1.3 gather_fusion.4
  17.5 0.9 gather_fusion.5
  18.4 1.3 gather_fusion.9
  19.7 0.7 broadcast_select_fusion.3
  20.5 0.8 broadcast_select_fusion.1
  21.3 0.7 broadcast_select_fusion.2
  22.0 0.8 broadcast_select_fusion
  22.8 0.0 reduce-scatter.3.cloned.1.call-start
  22.9 2.6 multiply_add_fusion.2
  25.4 1.0 gather_fusion.1
  26.4 1.2 gather_fusion.2
  27.6 0.2 multiply_reduce_fusion
  27.8 140.3 %all-reduce.5.cloned.1.call-done = (bf16[256,128]{1,0:T(8,128)(2,1)}, bf16[512,128]{1,0:T(8,128)(2,1)}, bf16[256,128]{1,0:T(8,128)(2,1)}, bf16[512,128]{1,0:T(8,128)(2,1)}) async-done(((bf16[256,128]{1,0:T(8,128)(2,1)}, bf16[512,128]{1,0:T(8,128)(2,1)}, bf16[256,128]{1,0:T(8,128)(2,1)}, bf16[512,128]{1,0:T(8,128)(2,1)}), (bf16[256,128]{1,0:T(8,128)(2,1)}, bf16[512,128]{1,0:T(8,128)(2,1)}, ...) | async-done | bytes 393232 | tf_op jit(solution)/shard_map/psum | solution.py:78
  168.1 0.9 multiply_reduce_fusion.4
  169.0 2.1 fusion.16
  171.2 0.0 all-gather.3.cloned.1.call-start
  171.2 0.8 multiply_reduce_fusion.6
  172.0 0.1 multiply_reduce_fusion.2
  172.2 0.8 fusion.24
  173.0 210.5 %reduce-scatter.3.cloned.1.call-done = f32[8,256]{1,0:T(8,128)} async-done(((f32[256,256]{1,0:T(8,128)}), f32[8,256]{1,0:T(8,128)}) %reduce-scatter.3.cloned.1.call-update) | async-done | bytes 8208 | tf_op jit(solution)/shard_map/reduce_scatter | solution.py:93
  383.5 1.0 fusion.60
  384.6 83.0 %all-reduce.6 = bf16[512,256]{1,0:T(8,128)(2,1)S(1)} all-reduce(f32[512,256]{1,0:T(8,128)S(1)} %fusion.60), channel_id=1, replica_groups=mesh['rows'=8,'pts'=32] {'rows','pts'}, use_global_device_ids=true, to_apply=%region_7.8 | all-reduce | flops 131072 | bytes 786432 | tf_op jit(solution)/shard_map/psum | solution.py:96
  467.6 2.1 fusion.28
  469.7 0.0 reduce-scatter.5.cloned.1.call-start
  469.8 1.2 gather_fusion.7
  471.0 0.1 multiply_reduce_fusion.3
  471.1 98.4 %all-gather.3.cloned.1.call-done = bf16[2048,256]{1,0:T(8,128)(2,1)} async-done(((bf16[8,256]{1,0:T(8,128)(2,1)}), bf16[2048,256]{1,0:T(8,128)(2,1)}) %all-gather.3.cloned.1.call-update) | async-done | bytes 1048592 | tf_op jit(solution)/shard_map/all_gather | solution.py:98
  569.5 12.7 %scatter_custom_fusion.1 = f32[1024,256]{1,0:T(8,128)S(1)} fusion(f32[1024,256]{1,0:T(8,128)S(1)} %get-tuple-element.9, s32[2048]{0:T(1024)S(1)} %bitcast.54, bf16[2048,256]{1,0:T(8,128)(2,1)} %all-gather.3.cloned.1.call-done, f32[]{:T(128)} %constant.14.clone.1), kind=kCustom, calls=%fused_computation.19 | custom fusion | flops 1572864 | bytes 2097156 | tf_op jit(solution)/shard_map/scatter-add | solution.py:100
  582.2 13.8 %scatter_custom_fusion = f32[1024,256]{1,0:T(8,128)} fusion(f32[1024,256]{1,0:T(8,128)} %get-tuple-element.8, s32[2048]{0:T(1024)S(1)} %bitcast.55, bf16[2048,256]{1,0:T(8,128)(2,1)S(1)} %copy-done.3, f32[]{:T(128)} %constant.13.clone.1), kind=kCustom, calls=%fused_computation.18 | custom fusion | flops 1572864 | bytes 2097664 | tf_op jit(solution)/shard_map/scatter-add | solution.py:104
  596.0 2.5 multiply_add_fusion
  598.4 1.0 gather_fusion.6
  599.4 1.3 fusion.17
  600.7 0.0 all-gather.5.cloned.1.call-start
  600.8 0.1 multiply_reduce_fusion.5
  600.9 0.1 multiply_reduce_fusion.1
  601.0 0.2 fusion.25
  601.2 206.7 %reduce-scatter.5.cloned.1.call-done = f32[8,256]{1,0:T(8,128)} async-done(((f32[256,256]{1,0:T(8,128)}), f32[8,256]{1,0:T(8,128)}) %reduce-scatter.5.cloned.1.call-update) | async-done | bytes 8208 | tf_op jit(solution)/shard_map/reduce_scatter | solution.py:93
  807.9 1.0 fusion.58
  808.9 82.9 %all-reduce.7 = bf16[512,256]{1,0:T(8,128)(2,1)S(1)} all-reduce(f32[512,256]{1,0:T(8,128)S(1)} %fusion.58), channel_id=1, replica_groups=mesh['rows'=8,'pts'=32] {'rows','pts'}, use_global_device_ids=true, to_apply=%region_16.17 | all-reduce | flops 131072 | bytes 786432 | tf_op jit(solution)/shard_map/psum | solution.py:96
  891.9 2.1 fusion.29
  894.0 99.8 %all-gather.5.cloned.1.call-done = bf16[2048,256]{1,0:T(8,128)(2,1)} async-done(((bf16[8,256]{1,0:T(8,128)(2,1)}), bf16[2048,256]{1,0:T(8,128)(2,1)}) %all-gather.5.cloned.1.call-update) | async-done | bytes 1048592 | tf_op jit(solution)/shard_map/all_gather | solution.py:98
  993.8 12.5 %scatter_custom_fusion.2 = f32[1024,256]{1,0:T(8,128)S(1)} fusion(f32[1024,256]{1,0:T(8,128)S(1)} %get-tuple-element.7, s32[2048]{0:T(1024)S(1)} %bitcast.52, bf16[2048,256]{1,0:T(8,128)(2,1)} %all-gather.5.cloned.1.call-done, f32[]{:T(128)} %constant.14.clone.1), kind=kCustom, calls=%fused_computation.20 | custom fusion | flops 1572864 | bytes 2097156 | tf_op jit(solution)/shard_map/scatter-add | solution.py:100
  1006.3 14.1 %scatter_custom_fusion.3 = f32[1024,256]{1,0:T(8,128)} fusion(f32[1024,256]{1,0:T(8,128)} %get-tuple-element.6, s32[2048]{0:T(1024)S(1)} %bitcast.53, bf16[2048,256]{1,0:T(8,128)(2,1)S(1)} %copy-done.4, f32[]{:T(128)} %constant.13.clone.1), kind=kCustom, calls=%fused_computation.21 | custom fusion | flops 1572864 | bytes 2097664 | tf_op jit(solution)/shard_map/scatter-add | solution.py:104
  (43 shorter events, 0.3 us)
Async XLA Ops:
  7.2 19.2 %copy-start = (bf16[1024,256]{1,0:T(8,128)(2,1)S(1)}, bf16[1024,256]{1,0:T(8,128)(2,1)}, u32[]{:S(2)}) copy-start(bf16[1024,256]{1,0:T(8,128)(2,1)} %param.8) | copy-start | bytes 1572868
  7.2 160.9 %all-reduce.5.cloned.1.call-start = ((), (), s32[]{:S(2)}) async-start(), calls=%async_computation.6 | async-start | bytes 786432 | tf_op jit(solution)/shard_map/psum | solution.py:78
  12.1 3.2 copy-start.1
  18.4 4.5 copy-start.5
  22.8 360.7 %reduce-scatter.3.cloned.1.call-start = ((), (), s32[]{:S(2)}) async-start(), calls=%async_computation.2 | async-start | bytes 270336 | tf_op jit(solution)/shard_map/reduce_scatter | solution.py:93
  169.0 3.0 copy-start.7
  171.2 398.3 %all-gather.3.cloned.1.call-start = ((), (), s32[]{:S(2)}) async-start(), calls=%async_computation.3 | async-start | bytes 1052672 | tf_op jit(solution)/shard_map/all_gather | solution.py:98
  383.5 84.0 %copy-start.10 = (f32[8,256]{1,0:T(8,128)S(1)}, f32[8,256]{1,0:T(8,128)}, u32[]{:S(2)}) copy-start(f32[8,256]{1,0:T(8,128)} %reduce-scatter.3.cloned.1.call-done) | copy-start | bytes 24580
  467.5 3.4 copy-start.9
  467.5 3.4 copy-start.8
  469.7 338.1 %reduce-scatter.5.cloned.1.call-start = ((), (), s32[]{:S(2)}) async-start(), calls=%async_computation.4 | async-start | bytes 270336 | tf_op jit(solution)/shard_map/reduce_scatter | solution.py:93
  569.5 12.7 %copy-start.3 = (bf16[2048,256]{1,0:T(8,128)(2,1)S(1)}, bf16[2048,256]{1,0:T(8,128)(2,1)}, u32[]{:S(2)}) copy-start(bf16[2048,256]{1,0:T(8,128)(2,1)} %all-gather.3.cloned.1.call-done) | copy-start | bytes 3145732
  599.4 1.5 copy-start.6
  600.7 393.1 %all-gather.5.cloned.1.call-start = ((), (), s32[]{:S(2)}) async-start(), calls=%async_computation.5 | async-start | bytes 1052672 | tf_op jit(solution)/shard_map/all_gather | solution.py:98
  807.9 84.0 %copy-start.11 = (f32[8,256]{1,0:T(8,128)S(1)}, f32[8,256]{1,0:T(8,128)}, u32[]{:S(2)}) copy-start(f32[8,256]{1,0:T(8,128)} %reduce-scatter.5.cloned.1.call-done) | copy-start | bytes 24580
  993.8 12.5 %copy-start.4 = (bf16[2048,256]{1,0:T(8,128)(2,1)S(1)}, bf16[2048,256]{1,0:T(8,128)(2,1)}, u32[]{:S(2)}) copy-start(bf16[2048,256]{1,0:T(8,128)(2,1)} %all-gather.5.cloned.1.call-done) | copy-start | bytes 3145732
  1006.3 14.2 %copy-start.2 = (f32[1024,256]{1,0:T(8,128)}, f32[1024,256]{1,0:T(8,128)S(1)}, u32[]{:S(2)}) copy-start(f32[1024,256]{1,0:T(8,128)S(1)} %scatter_custom_fusion.2) | copy-start | bytes 3145732
Sparse Core Ops, SparseCore 0:
  22.9 145.1 all-reduce.4
  172.9 210.5 reduce-scatter.2
  469.8 99.5 all-gather.2
  600.8 206.9 reduce-scatter.4
  894.1 99.5 all-gather.4
where the time goes:
time: 1030 us
  waiting for transfers between devices  756 us (73%)
  blocking collectives  166 us (16%)
  other arithmetic  64.6 us (6%)
  local copies, waits for them, and re-layouts  15.8 us (2%)
  between operations  14.1 us (1%)
  matrix products  10.7 us (1%)
    reduce_scatter x2, waiting for transfers between devices, shards(): lax.psum_scatter(partial_value, 'pts', scatter_dimension=0, tiled=True)  417 us
    all_gather x2, waiting for transfers between devices, shards(): steps = lax.all_gather(step_bf, ('rows', 'pts'), axis=0, tiled=True)  198 us
    psum x2, blocking collectives, shards(): proj = lax.psum(project_rows(factor, resid), ('rows', 'pts'))  166 us
    psum x1, waiting for transfers between devices, shards(): lax.psum(row_terms, 'pts').astype(jnp.float32)  140 us
    scatter-add x2, other arithmetic, shards(): momentum_now = (beta_keep * momentum_now + (1.0 - beta_keep) * mixed).at[...  27.9 us
    scatter-add x2, other arithmetic, shards(): current = mixed.at[whole_slots].add(-step_size * change, mode='drop')  25.2 us
  transfers between devices with their start and end apart: 5, of which 5 were waited for; matrix products, arithmetic and copies ran while one was open for 1% of the time, Pallas kernels for 0%

commit v1 on v0

--- a/solution.py
+++ b/solution.py
@@ -75,7 +75,7 @@
             pivot_holder[:, None], features[pivot_pos], jnp.zeros((), jnp.bfloat16)
         )
         got_rows, got_pivots = (
-            lax.psum(row_terms, "pts").astype(jnp.float32),
+            jnp.sum(lax.all_gather(row_terms, "pts"), axis=0).astype(jnp.float32),
             lax.psum(pivot_terms, "pts").astype(jnp.float32),
         )
         block_feats = got_rows.astype(jnp.bfloat16)

time: 1030 us -> 1100 us (1.068)
  waiting for transfers between devices: 756 us -> 819 us
    all_gather x0 -> x2, waiting for transfers between devices: none -> 62 us  [shards(): lax.all_gather(row_terms, 'pts')]
  transfers between devices with their start and end apart: 5 -> 7, of which waited for: 5 -> 6; matrix products, arithmetic and copies ran while one was open for 1% -> 3% of each run, Pallas kernels for 0% -> 0%
where the time goes in v1:
time: 1100 us; the launch traced here: 1090 us
  waiting for transfers between devices  819 us (74%)
  blocking collectives  166 us (15%)
  other arithmetic  67.9 us (6%)
  local copies, waits for them, and re-layouts  16.6 us (2%)
  between operations  14.4 us (1%)
    reduce_scatter x2, waiting for transfers between devices, shards(): lax.psum_scatter(partial_value, 'pts', scatter_dimension=0, tiled=True)  419 us
    all_gather x2, waiting for transfers between devices, shards(): steps = lax.all_gather(step_bf, ('rows', 'pts'), axis=0, tiled=True)  199 us
    psum x2, blocking collectives, shards(): proj = lax.psum(project_rows(factor, resid), ('rows', 'pts'))  166 us
    psum x1, waiting for transfers between devices, shards(): lax.psum(pivot_terms, 'pts').astype(jnp.float32)  139 us
    all_gather x2, waiting for transfers between devices, shards(): lax.all_gather(row_terms, 'pts')  62 us
    scatter-add x2, other arithmetic, shards(): momentum_now = (beta_keep * momentum_now + (1.0 - beta_keep) * mixed).at[...  27.9 us
    scatter-add x2, other arithmetic, shards(): current = mixed.at[whole_slots].add(-step_size * change, mode='drop')  25.2 us
  transfers between devices with their start and end apart: 7, of which 6 were waited for; matrix products, arithmetic and copies ran while one was open for 3% of the time, Pallas kernels for 0%

profile of v1, /device:TPU:1, one launch (start us, length us, event | category | flops | bytes accessed | tf_op | source)
XLA Modules:
  0.0 1094.7 jit_solution(5457746668767336909)
XLA Ops:
  7.2 0.8 fusion.70
  8.1 1.7 gather_fusion
  9.8 0.7 bitcast_select_fusion.1
  10.6 0.8 compare_select_fusion.3
  11.4 3.1 gather_fusion.8
  14.6 3.1 gather_fusion.3
  17.8 1.3 gather_fusion.4
  19.2 1.3 gather_fusion.9
  20.5 0.8 broadcast_select_fusion.1
  21.3 0.8 broadcast_select_fusion
  22.1 0.0 reduce-scatter.3.cloned.1.call-start
  22.2 0.2 multiply_reduce_fusion
  22.4 2.6 multiply_add_fusion.2
  25.0 1.0 gather_fusion.1
  25.9 1.2 gather_fusion.2
  27.1 62.0 %all-gather.5.cloned.1.call-done = bf16[32,256,128]{2,1,0:T(8,128)(2,1)} async-done(((bf16[1,256,128]{2,1,0:T(8,128)(2,1)}), bf16[32,256,128]{2,1,0:T(8,128)(2,1)}) %all-gather.5.cloned.1.call-update) | async-done | bytes 2097168 | tf_op jit(solution)/shard_map/all_gather | solution.py:78
  89.1 1.9 reduce_sum.91
  91.0 0.1 multiply_reduce_fusion.4
  91.1 1.3 fusion.16
  92.4 0.9 gather_fusion.5
  93.3 0.7 bitcast_select_fusion
  94.1 139.4 %all-reduce.5.cloned.1.call-done = (bf16[512,128]{1,0:T(8,128)(2,1)}, bf16[512,128]{1,0:T(8,128)(2,1)}) async-done(((bf16[512,128]{1,0:T(8,128)(2,1)}, bf16[512,128]{1,0:T(8,128)(2,1)}), (bf16[512,128]{1,0:T(8,128)(2,1)}, bf16[512,128]{1,0:T(8,128)(2,1)})) %all-reduce.5.cloned.1.call-update) | async-done | bytes 262160 | tf_op jit(solution)/shard_map/psum | solution.py:79
  233.5 1.0 multiply_reduce_fusion.2
  234.6 0.1 multiply_reduce_fusion.6
  234.7 1.1 fusion.24
  235.8 212.3 %reduce-scatter.3.cloned.1.call-done = f32[8,256]{1,0:T(8,128)} async-done(((f32[256,256]{1,0:T(8,128)}), f32[8,256]{1,0:T(8,128)}) %reduce-scatter.3.cloned.1.call-update) | async-done | bytes 8208 | tf_op jit(solution)/shard_map/reduce_scatter | solution.py:93
  448.1 1.0 fusion.60
  449.0 83.4 %all-reduce.6 = bf16[512,256]{1,0:T(8,128)(2,1)S(1)} all-reduce(f32[512,256]{1,0:T(8,128)S(1)} %fusion.60), channel_id=1, replica_groups=mesh['rows'=8,'pts'=32] {'rows','pts'}, use_global_device_ids=true, to_apply=%region_7.8 | all-reduce | flops 131072 | bytes 786432 | tf_op jit(solution)/shard_map/psum | solution.py:96
  532.5 2.1 fusion.28
  534.6 1.2 gather_fusion.7
  535.9 1.9 reduce_sum.96
  537.8 0.1 multiply_reduce_fusion.3
  537.9 98.9 %all-gather.7.cloned.1.call-done = bf16[2048,256]{1,0:T(8,128)(2,1)} async-done(((bf16[8,256]{1,0:T(8,128)(2,1)}), bf16[2048,256]{1,0:T(8,128)(2,1)}) %all-gather.7.cloned.1.call-update) | async-done | bytes 1048592 | tf_op jit(solution)/shard_map/all_gather | solution.py:98
  636.8 12.7 %scatter_custom_fusion.1 = f32[1024,256]{1,0:T(8,128)S(1)} fusion(f32[1024,256]{1,0:T(8,128)S(1)} %get-tuple-element.7, s32[2048]{0:T(1024)S(1)} %bitcast.58, bf16[2048,256]{1,0:T(8,128)(2,1)} %all-gather.7.cloned.1.call-done, f32[]{:T(128)} %constant.16.clone.1), kind=kCustom, calls=%fused_computation.19 | custom fusion | flops 1572864 | bytes 2097156 | tf_op jit(solution)/shard_map/scatter-add | solution.py:100
  649.6 13.8 %scatter_custom_fusion = f32[1024,256]{1,0:T(8,128)} fusion(f32[1024,256]{1,0:T(8,128)} %get-tuple-element.6, s32[2048]{0:T(1024)S(1)} %bitcast.59, bf16[2048,256]{1,0:T(8,128)(2,1)S(1)} %copy-done.3, f32[]{:T(128)} %constant.15.clone.1), kind=kCustom, calls=%fused_computation.18 | custom fusion | flops 1572864 | bytes 2097664 | tf_op jit(solution)/shard_map/scatter-add | solution.py:104
  663.3 2.6 multiply_add_fusion
  665.9 1.0 gather_fusion.6
  666.9 1.3 fusion.17
  668.2 0.1 multiply_reduce_fusion.1
  668.3 0.1 multiply_reduce_fusion.5
  668.5 0.2 fusion.25
  668.6 206.6 %reduce-scatter.5.cloned.1.call-done = f32[8,256]{1,0:T(8,128)} async-done(((f32[256,256]{1,0:T(8,128)}), f32[8,256]{1,0:T(8,128)}) %reduce-scatter.5.cloned.1.call-update) | async-done | bytes 8208 | tf_op jit(solution)/shard_map/reduce_scatter | solution.py:93
  875.3 1.0 fusion.58
  876.2 83.0 %all-reduce.7 = bf16[512,256]{1,0:T(8,128)(2,1)S(1)} all-reduce(f32[512,256]{1,0:T(8,128)S(1)} %fusion.58), channel_id=1, replica_groups=mesh['rows'=8,'pts'=32] {'rows','pts'}, use_global_device_ids=true, to_apply=%region_16.17 | all-reduce | flops 131072 | bytes 786432 | tf_op jit(solution)/shard_map/psum | solution.py:96
  959.2 2.1 fusion.29
  961.3 99.8 %all-gather.11.cloned.1.call-done = bf16[2048,256]{1,0:T(8,128)(2,1)} async-done(((bf16[8,256]{1,0:T(8,128)(2,1)}), bf16[2048,256]{1,0:T(8,128)(2,1)}) %all-gather.11.cloned.1.call-update) | async-done | bytes 1048592 | tf_op jit(solution)/shard_map/all_gather | solution.py:98
  1061.2 12.5 %scatter_custom_fusion.2 = f32[1024,256]{1,0:T(8,128)S(1)} fusion(f32[1024,256]{1,0:T(8,128)S(1)} %get-tuple-element.5, s32[2048]{0:T(1024)S(1)} %bitcast.56, bf16[2048,256]{1,0:T(8,128)(2,1)} %all-gather.11.cloned.1.call-done, f32[]{:T(128)} %constant.16.clone.1), kind=kCustom, calls=%fused_computation.20 | custom fusion | flops 1572864 | bytes 2097156 | tf_op jit(solution)/shard_map/scatter-add | solution.py:100
  1073.7 14.1 %scatter_custom_fusion.3 = f32[1024,256]{1,0:T(8,128)} fusion(f32[1024,256]{1,0:T(8,128)} %get-tuple-element.4, s32[2048]{0:T(1024)S(1)} %bitcast.57, bf16[2048,256]{1,0:T(8,128)(2,1)S(1)} %copy-done.4, f32[]{:T(128)} %constant.15.clone.1), kind=kCustom, calls=%fused_computation.21 | custom fusion | flops 1572864 | bytes 2097664 | tf_op jit(solution)/shard_map/scatter-add | solution.py:104
  (45 shorter events, 0.6 us)
Async XLA Ops:
  7.2 18.8 %copy-start = (bf16[1024,256]{1,0:T(8,128)(2,1)S(1)}, bf16[1024,256]{1,0:T(8,128)(2,1)}, u32[]{:S(2)}) copy-start(bf16[1024,256]{1,0:T(8,128)(2,1)} %param.8) | copy-start | bytes 1572868
  7.2 81.9 %all-gather.5.cloned.1.call-start = ((), (), s32[]{:S(2)}) async-start(), calls=%async_computation.2 | async-start | bytes 2162688 | tf_op jit(solution)/shard_map/all_gather | solution.py:78
  10.6 222.9 %all-reduce.5.cloned.1.call-start = ((), (), s32[]{:S(2)}) async-start(), calls=%async_computation.8 | async-start | bytes 524288 | tf_op jit(solution)/shard_map/psum | solution.py:79
  11.4 6.4 copy-start.1
  17.7 4.7 copy-start.5
  22.1 425.9 %reduce-scatter.3.cloned.1.call-start = ((), (), s32[]{:S(2)}) async-start(), calls=%async_computation.3 | async-start | bytes 270336 | tf_op jit(solution)/shard_map/reduce_scatter | solution.py:93
  92.4 443.5 %all-gather.9.cloned.1.call-start = ((), (), s32[]{:S(2)}) async-start(), calls=%async_computation.5 | async-start | bytes 2162688 | tf_op jit(solution)/shard_map/all_gather | solution.py:78
  93.3 442.5 %copy-start.7 = (s32[2,2048]{1,0:T(2,128)S(1)}, s32[2,2048]{1,0:T(2,128)}, u32[]{:S(2)}) copy-start(s32[2,2048]{1,0:T(2,128)} %param.11) | copy-start | bytes 49156
  94.1 542.8 %all-gather.7.cloned.1.call-start = ((), (), s32[]{:S(2)}) async-start(), calls=%async_computation.4 | async-start | bytes 1052672 | tf_op jit(solution)/shard_map/all_gather | solution.py:98
  534.6 340.7 %reduce-scatter.5.cloned.1.call-start = ((), (), s32[]{:S(2)}) async-start(), calls=%async_computation.6 | async-start | bytes 270336 | tf_op jit(solution)/shard_map/reduce_scatter | solution.py:93
  636.8 12.7 %copy-start.3 = (bf16[2048,256]{1,0:T(8,128)(2,1)S(1)}, bf16[2048,256]{1,0:T(8,128)(2,1)}, u32[]{:S(2)}) copy-start(bf16[2048,256]{1,0:T(8,128)(2,1)} %all-gather.7.cloned.1.call-done) | copy-start | bytes 3145732
  665.9 2.3 copy-start.6
  668.1 393.0 %all-gather.11.cloned.1.call-start = ((), (), s32[]{:S(2)}) async-start(), calls=%async_computation.7 | async-start | bytes 1052672 | tf_op jit(solution)/shard_map/all_gather | solution.py:98
  1061.2 12.5 %copy-start.4 = (bf16[2048,256]{1,0:T(8,128)(2,1)S(1)}, bf16[2048,256]{1,0:T(8,128)(2,1)}, u32[]{:S(2)}) copy-start(bf16[2048,256]{1,0:T(8,128)(2,1)} %all-gather.11.cloned.1.call-done) | copy-start | bytes 3145732
  1073.7 14.2 %copy-start.2 = (f32[1024,256]{1,0:T(8,128)}, f32[1024,256]{1,0:T(8,128)S(1)}, u32[]{:S(2)}) copy-start(f32[1024,256]{1,0:T(8,128)S(1)} %scatter_custom_fusion.2) | copy-start | bytes 3145732
Sparse Core Ops, SparseCore 0:
  11.2 77.8 all-gather.4
  92.6 140.8 all-reduce.4
  237.9 210.1 reduce-scatter.2
  450.8 77.5 all-gather.8
  534.7 102.0 all-gather.6
  668.3 206.9 reduce-scatter.4
  961.5 99.6 all-gather.10
